TPU v7x, 32 devices: a whole 2x2x4 slice. The times are simulated.
32 devices in a mesh: node: 8 (over z, x), rep: 4 (over y, core).
Axes of the slice: x: 2, y: 2, z: 4, core: 2. Of those that a mesh axis runs over, the one named last changes fastest.
Arguments:
- features: bfloat16 [8192, 512], P(('node', 'rep')), may hold values from -6 to 6
- weight: bfloat16 [512, 512], replicated, may hold values from -0.25 to 0.25
- cotangent: bfloat16 [8192, 512], P(('node', 'rep')), may hold values from -6 to 6
- tile_values: bfloat16 [8192, 128, 128], P(('node', 'rep')), may hold values from -0.125 to 0.125
- tile_row: int32 [8192], P(('node', 'rep')), may hold values from 0 to 7
- tile_col: int32 [8192], P(('node', 'rep')), may hold values from 0 to 15
- tile_count: int32 [32], P(('node', 'rep')), may hold values from 64 to 256, as said below
Outputs:
- activation: bfloat16 [8192, 512], P(('node', 'rep'))
- weight_grad: float32 [512, 512], replicated
- feature_grad: bfloat16 [8192, 512], P(('node', 'rep'))
Inputs may be any that keep to these rules, and one draw needn't show every extreme that they name: `tile_count`: slots of a device below its count hold tiles, the others are ignored; some device uses all 256 slots.
All inputs are finite; a program needn't handle non-finite values.
Results may differ from a plain program's by a relative error of at most 0.023.
Values may be sent and summed in bfloat16 or wider, within the bound.
A program may use at most 128 MiB of HBM per device.

v0:
```python
import math
import jax
import jax.numpy as jnp
from jax import lax
from jax.sharding import PartitionSpec as P

TB = 128


def smooth_gate(values):
    return jax.nn.gelu(values, approximate=True)


def apply_tiles(
    tile_values, tile_row, tile_col, tile_count, sources, target_shape, backward, window_start
):
    group_size = min(32, tile_row.shape[0])
    filled = tile_count[0]
    turns_needed = (filled + group_size - 1) // group_size
    window_blocks = target_shape[0]

    def one_turn(turn_index, totals):
        offset = turn_index * group_size
        values = lax.dynamic_slice_in_dim(tile_values, offset, group_size, 0)
        rows_here = lax.dynamic_slice_in_dim(tile_row, offset, group_size, 0)
        cols_here = lax.dynamic_slice_in_dim(tile_col, offset, group_size, 0)
        slot_mask = (offset + jnp.arange(group_size, dtype=jnp.int32) < filled).astype(jnp.float32)
        if backward:
            local_cols = cols_here - window_start
            inside = ((local_cols >= 0) & (local_cols < window_blocks)).astype(jnp.float32)
            placed = jnp.clip(local_cols, 0, window_blocks - 1)
            product = jnp.einsum(
                "tji,tjf->tif", values, sources[rows_here], preferred_element_type=jnp.float32
            )
            return totals.at[placed].add(product * (slot_mask * inside)[:, None, None])
        product = jnp.einsum(
            "tij,tjf->tif", values, sources[cols_here], preferred_element_type=jnp.float32
        )
        return totals.at[rows_here].add(product * slot_mask[:, None, None])

    return lax.fori_loop(0, turns_needed, one_turn, jnp.zeros(target_shape, jnp.float32))


def local(features, weight, cotangent, tile_values, tile_row, tile_col, tile_count):
    rows_quarter = features.shape[0]
    feature_width = features.shape[1]
    rep_count = lax.axis_size("rep")
    node_count = lax.axis_size("node")
    scale = 1.0 / math.sqrt(rows_quarter * rep_count * node_count)
    gathered = lax.all_gather(features, "node", axis=0, tiled=True)
    source_blocks = gathered.reshape(-1, TB, feature_width)
    block_count = rows_quarter * rep_count // TB
    partial_value = apply_tiles(
        tile_values,
        tile_row,
        tile_col,
        tile_count,
        source_blocks,
        (block_count, TB, feature_width),
        False,
        0,
    ).reshape(block_count * TB, feature_width)
    aggregate_all = lax.psum(partial_value, "rep").astype(jnp.bfloat16)
    cotangent_all = lax.all_gather(cotangent, "rep", axis=0, tiled=True)
    pre = jnp.dot(aggregate_all, weight, preferred_element_type=jnp.float32)
    activated, pullback = jax.vjp(smooth_gate, pre)
    grad_all = pullback(cotangent_all.astype(jnp.float32))[0].astype(jnp.bfloat16)
    full_grad = jnp.dot(grad_all, weight.T, preferred_element_type=jnp.float32).astype(jnp.bfloat16)
    offset = lax.axis_index("rep") * rows_quarter
    own_aggregate = lax.dynamic_slice_in_dim(aggregate_all, offset, rows_quarter, 0)
    own_grad = lax.dynamic_slice_in_dim(grad_all, offset, rows_quarter, 0)
    weight_term = jnp.dot(own_aggregate.T, own_grad, preferred_element_type=jnp.float32)
    output_rows = lax.dynamic_slice_in_dim(activated, offset, rows_quarter, 0).astype(jnp.bfloat16)
    weight_grad = lax.psum(weight_term, ("node", "rep")) * scale
    grad_blocks = full_grad.reshape(block_count, TB, feature_width)
    contributions = apply_tiles(
        tile_values, tile_row, tile_col, tile_count, grad_blocks, source_blocks.shape, True, 0
    )
    feature_grad = lax.psum_scatter(
        contributions.reshape(-1, feature_width).astype(jnp.bfloat16),
        "node",
        scatter_dimension=0,
        tiled=True,
    )
    return (output_rows, weight_grad, feature_grad)


def solution(mesh):
    in_specs = (
        P(("node", "rep"), None),
        P(),
        P(("node", "rep"), None),
        P(("node", "rep"), None, None),
        P(("node", "rep")),
        P(("node", "rep")),
        P(("node", "rep")),
    )
    out_specs = (P(("node", "rep"), None), P(), P(("node", "rep"), None))
    return jax.shard_map(local, mesh=mesh, in_specs=in_specs, out_specs=out_specs, check_vma=False)
```

profile of v0, /device:TPU:0, one launch (start us, length us, event | category | flops | bytes accessed | tf_op | source)
XLA Modules:
  0.0 611.5 jit_solution(17007301135434615890)
XLA Ops:
  7.2 0.0 copy-start
  7.2 0.0 copy-start.1
  7.2 0.0 all-gather.3.cloned.1.call-start
  7.2 0.7 all-gather.3.cloned.1.call-update
  7.9 0.0 all-gather.5.cloned.1.call-start
  8.0 0.7 all-gather.5.cloned.1.call-update
  8.7 0.0 all-reduce.3.cloned.1.call-start
  9.4 52.6 %all-gather.3.cloned.1.call-done = bf16[2048,512]{1,0:T(8,128)(2,1)} async-done(((bf16[256,512]{1,0:T(8,128)(2,1)}), bf16[2048,512]{1,0:T(8,128)(2,1)}) %all-gather.3.cloned.1.call-update) | async-done | bytes 2097168 | tf_op jit(solution)/shard_map/all_gather | solution.py:50
  62.0 0.2 broadcast_in_dim.20
  62.3 95.9 %while.20 = (s32[]{:T(128)}, f32[8,128,512]{2,1,0:T(8,128)S(1)}, s32[]{:T(128)}, s32[256]{0:T(256)S(1)}, bf16[256,128,128]{2,1,0:T(8,128)(2,1)}, /*index=5*/s32[...) while((s32[]{:T(128)}, f32[8,128,512]{2,1,0:T(8,128)S(1)}, ...), condition=%wide.region_2.3_spmd, body=%wide.region_0.2_spmd.sunk | while | flops 541066560 | bytes 47191344 | solution.py:41
  62.3 0.7 compare_convert_fusion.3
  62.9 0.1 compare_select_fusion.6
  63.0 4.4 gather_fusion
  67.4 7.2 %broadcast_multiply_fusion.5 = f32[32,128,512]{2,1,0:T(8,128)} fusion(f32[32]{0:T(128)S(1)} %compare_convert_fusion.3, bf16[32,128,512]{2,1,0:T(8,128)(2,1)} %gather_fusion, bf16[256,128,128]{2,1,0:T(8,128)(2,1)} %get-tuple-element.274, s32[]{:T(128)S(6)} %select_n.44), kind=kOutput, calls=%fused_computation.4.clone.1 | convolution fusion | flops 538968064 | bytes 13631620 | tf_op jit(solution)/shard_map/while/body/tij,tjf->tif/dot_general | solution.py:36
  74.6 11.8 %scatter_fusion = f32[8,128,512]{2,1,0:T(8,128)S(1)} fusion(f32[8,128,512]{2,1,0:T(8,128)S(1)} %get-tuple-element.259, s32[32]{0:T(128)S(1)} %get-tuple-element.234, f32[32,128,512]{2,1,0:T(8,128)} %broadcast_multiply_fusion.5), kind=kCustom, calls=%fused_computation.2.clone.1 | custom fusion | flops 2097152 | bytes 25165952 | tf_op jit(solution)/shard_map/while/body/scatter-add | solution.py:39
  86.4 0.7 compare_convert_fusion.3
  87.1 0.1 compare_select_fusion.6
  87.2 4.4 gather_fusion
  91.5 7.0 %broadcast_multiply_fusion.5 = f32[32,128,512]{2,1,0:T(8,128)} fusion(f32[32]{0:T(128)S(1)} %compare_convert_fusion.3, bf16[32,128,512]{2,1,0:T(8,128)(2,1)} %gather_fusion, bf16[256,128,128]{2,1,0:T(8,128)(2,1)} %get-tuple-element.274, s32[]{:T(128)S(6)} %select_n.44), kind=kOutput, calls=%fused_computation.4.clone.1 | convolution fusion | flops 538968064 | bytes 13631620 | tf_op jit(solution)/shard_map/while/body/tij,tjf->tif/dot_general | solution.py:36
  98.5 11.8 %scatter_fusion = f32[8,128,512]{2,1,0:T(8,128)S(1)} fusion(f32[8,128,512]{2,1,0:T(8,128)S(1)} %get-tuple-element.259, s32[32]{0:T(128)S(1)} %get-tuple-element.234, f32[32,128,512]{2,1,0:T(8,128)} %broadcast_multiply_fusion.5), kind=kCustom, calls=%fused_computation.2.clone.1 | custom fusion | flops 2097152 | bytes 25165952 | tf_op jit(solution)/shard_map/while/body/scatter-add | solution.py:39
  110.3 0.7 compare_convert_fusion.3
  111.0 0.1 compare_select_fusion.6
  111.1 4.4 gather_fusion
  115.4 7.0 %broadcast_multiply_fusion.5 = f32[32,128,512]{2,1,0:T(8,128)} fusion(f32[32]{0:T(128)S(1)} %compare_convert_fusion.3, bf16[32,128,512]{2,1,0:T(8,128)(2,1)} %gather_fusion, bf16[256,128,128]{2,1,0:T(8,128)(2,1)} %get-tuple-element.274, s32[]{:T(128)S(6)} %select_n.44), kind=kOutput, calls=%fused_computation.4.clone.1 | convolution fusion | flops 538968064 | bytes 13631620 | tf_op jit(solution)/shard_map/while/body/tij,tjf->tif/dot_general | solution.py:36
  122.4 11.7 %scatter_fusion = f32[8,128,512]{2,1,0:T(8,128)S(1)} fusion(f32[8,128,512]{2,1,0:T(8,128)S(1)} %get-tuple-element.259, s32[32]{0:T(128)S(1)} %get-tuple-element.234, f32[32,128,512]{2,1,0:T(8,128)} %broadcast_multiply_fusion.5), kind=kCustom, calls=%fused_computation.2.clone.1 | custom fusion | flops 2097152 | bytes 25165952 | tf_op jit(solution)/shard_map/while/body/scatter-add | solution.py:39
  134.2 0.7 compare_convert_fusion.3
  134.8 0.1 compare_select_fusion.6
  134.9 4.4 gather_fusion
  139.3 7.0 %broadcast_multiply_fusion.5 = f32[32,128,512]{2,1,0:T(8,128)} fusion(f32[32]{0:T(128)S(1)} %compare_convert_fusion.3, bf16[32,128,512]{2,1,0:T(8,128)(2,1)} %gather_fusion, bf16[256,128,128]{2,1,0:T(8,128)(2,1)} %get-tuple-element.274, s32[]{:T(128)S(6)} %select_n.44), kind=kOutput, calls=%fused_computation.4.clone.1 | convolution fusion | flops 538968064 | bytes 13631620 | tf_op jit(solution)/shard_map/while/body/tij,tjf->tif/dot_general | solution.py:36
  146.3 11.8 %scatter_fusion = f32[8,128,512]{2,1,0:T(8,128)S(1)} fusion(f32[8,128,512]{2,1,0:T(8,128)S(1)} %get-tuple-element.259, s32[32]{0:T(128)S(1)} %get-tuple-element.234, f32[32,128,512]{2,1,0:T(8,128)} %broadcast_multiply_fusion.5), kind=kCustom, calls=%fused_computation.2.clone.1 | custom fusion | flops 2097152 | bytes 25165952 | tf_op jit(solution)/shard_map/while/body/scatter-add | solution.py:39
  158.1 87.7 %all-reduce.4 = bf16[1024,512]{1,0:T(8,128)(2,1)} all-reduce(f32[1024,512]{1,0:T(8,128)S(1)} %bitcast.16), channel_id=1, replica_groups=mesh['node'=8,'rep'=4] {'rep'}, use_global_device_ids=true, to_apply=%region_3.4 | all-reduce | flops 524288 | bytes 3145728 | tf_op jit(solution)/shard_map/psum | solution.py:63
  245.8 5.3 fusion.6
  251.2 0.7 convolution_convert_fusion
  251.9 2.3 fusion.15
  254.2 0.0 all-reduce.3.cloned.1.call-update
  254.2 0.0 reduce-scatter.2.cloned.1.call-start
  254.3 2.5 broadcast_in_dim.21
  256.8 117.3 %while.21 = (s32[]{:T(128)}, f32[16,128,512]{2,1,0:T(8,128)}, s32[]{:T(128)}, s32[256]{0:T(256)S(1)}, bf16[256,128,128]{2,1,0:T(8,128)(2,1)}, /*index=5*/s32[256...) while((s32[]{:T(128)}, f32[16,128,512]{2,1,0:T(8,128)}, ...), condition=%wide.region_7.8_spmd, body=%wide.region_5.7_spmd.sunk | while | flops 541066688 | bytes 47191480 | solution.py:41
  256.8 0.7 and_select_fusion.2
  257.5 0.1 compare_select_fusion.7
  257.6 2.8 gather_fusion.1
  260.3 7.3 %broadcast_multiply_fusion.6 = f32[32,128,512]{2,1,0:T(8,128)} fusion(f32[32]{0:T(128)S(1)} %and_select_fusion.2, bf16[32,128,512]{2,1,0:T(8,128)(2,1)} %gather_fusion.1, bf16[256,128,128]{2,1,0:T(8,128)(2,1)} %get-tuple-element.310, s32[]{:T(128)S(6)} %select_n.46), kind=kOutput, calls=%fused_computation.11.clone.1 | convolution fusion | flops 538968064 | bytes 13631620 | tf_op jit(solution)/shard_map/while/body/tji,tjf->tif/dot_general | solution.py:32
  267.6 18.4 %scatter_fusion.1 = f32[16,128,512]{2,1,0:T(8,128)} fusion(f32[16,128,512]{2,1,0:T(8,128)} %get-tuple-element.295, s32[32]{0:T(128)S(1)} %get-tuple-element.244, f32[32,128,512]{2,1,0:T(8,128)} %broadcast_multiply_fusion.6), kind=kCustom, calls=%fused_computation.3.clone.1 | custom fusion | flops 2097152 | bytes 25165952 | tf_op jit(solution)/shard_map/while/body/scatter-add | solution.py:35
  286.0 0.7 and_select_fusion.2
  286.7 0.1 compare_select_fusion.7
  286.8 2.8 gather_fusion.1
  289.5 7.3 %broadcast_multiply_fusion.6 = f32[32,128,512]{2,1,0:T(8,128)} fusion(f32[32]{0:T(128)S(1)} %and_select_fusion.2, bf16[32,128,512]{2,1,0:T(8,128)(2,1)} %gather_fusion.1, bf16[256,128,128]{2,1,0:T(8,128)(2,1)} %get-tuple-element.310, s32[]{:T(128)S(6)} %select_n.46), kind=kOutput, calls=%fused_computation.11.clone.1 | convolution fusion | flops 538968064 | bytes 13631620 | tf_op jit(solution)/shard_map/while/body/tji,tjf->tif/dot_general | solution.py:32
  296.8 18.7 %scatter_fusion.1 = f32[16,128,512]{2,1,0:T(8,128)} fusion(f32[16,128,512]{2,1,0:T(8,128)} %get-tuple-element.295, s32[32]{0:T(128)S(1)} %get-tuple-element.244, f32[32,128,512]{2,1,0:T(8,128)} %broadcast_multiply_fusion.6), kind=kCustom, calls=%fused_computation.3.clone.1 | custom fusion | flops 2097152 | bytes 25165952 | tf_op jit(solution)/shard_map/while/body/scatter-add | solution.py:35
  315.5 0.7 and_select_fusion.2
  316.2 0.1 compare_select_fusion.7
  316.3 2.8 gather_fusion.1
  319.0 7.3 %broadcast_multiply_fusion.6 = f32[32,128,512]{2,1,0:T(8,128)} fusion(f32[32]{0:T(128)S(1)} %and_select_fusion.2, bf16[32,128,512]{2,1,0:T(8,128)(2,1)} %gather_fusion.1, bf16[256,128,128]{2,1,0:T(8,128)(2,1)} %get-tuple-element.310, s32[]{:T(128)S(6)} %select_n.46), kind=kOutput, calls=%fused_computation.11.clone.1 | convolution fusion | flops 538968064 | bytes 13631620 | tf_op jit(solution)/shard_map/while/body/tji,tjf->tif/dot_general | solution.py:32
  326.3 18.3 %scatter_fusion.1 = f32[16,128,512]{2,1,0:T(8,128)} fusion(f32[16,128,512]{2,1,0:T(8,128)} %get-tuple-element.295, s32[32]{0:T(128)S(1)} %get-tuple-element.244, f32[32,128,512]{2,1,0:T(8,128)} %broadcast_multiply_fusion.6), kind=kCustom, calls=%fused_computation.3.clone.1 | custom fusion | flops 2097152 | bytes 25165952 | tf_op jit(solution)/shard_map/while/body/scatter-add | solution.py:35
  344.7 0.7 and_select_fusion.2
  345.4 0.1 compare_select_fusion.7
  345.5 2.8 gather_fusion.1
  348.2 7.3 %broadcast_multiply_fusion.6 = f32[32,128,512]{2,1,0:T(8,128)} fusion(f32[32]{0:T(128)S(1)} %and_select_fusion.2, bf16[32,128,512]{2,1,0:T(8,128)(2,1)} %gather_fusion.1, bf16[256,128,128]{2,1,0:T(8,128)(2,1)} %get-tuple-element.310, s32[]{:T(128)S(6)} %select_n.46), kind=kOutput, calls=%fused_computation.11.clone.1 | convolution fusion | flops 538968064 | bytes 13631620 | tf_op jit(solution)/shard_map/while/body/tji,tjf->tif/dot_general | solution.py:32
  355.5 18.5 %scatter_fusion.1 = f32[16,128,512]{2,1,0:T(8,128)} fusion(f32[16,128,512]{2,1,0:T(8,128)} %get-tuple-element.295, s32[32]{0:T(128)S(1)} %get-tuple-element.244, f32[32,128,512]{2,1,0:T(8,128)} %broadcast_multiply_fusion.6), kind=kCustom, calls=%fused_computation.3.clone.1 | custom fusion | flops 2097152 | bytes 25165952 | tf_op jit(solution)/shard_map/while/body/scatter-add | solution.py:35
  374.1 3.8 convert_element_type.37
  377.9 0.0 reduce-scatter.2.cloned.1.call-update
  377.9 2.0 fusion.14
  379.9 49.0 %all-reduce.3.cloned.1.call-done = f32[512,512]{1,0:T(8,128)} async-done(((f32[512,512]{1,0:T(8,128)}), f32[512,512]{1,0:T(8,128)}) %all-reduce.3.cloned.1.call-update) | async-done | bytes 1048592 | tf_op jit(solution)/shard_map/psum | solution.py:74
  428.9 2.3 broadcast_multiply_fusion.2
  431.2 173.9 %reduce-scatter.2.cloned.1.call-done = bf16[256,512]{1,0:T(8,128)(2,1)} async-done(((bf16[2048,512]{1,0:T(8,128)(2,1)}), bf16[256,512]{1,0:T(8,128)(2,1)}) %reduce-scatter.2.cloned.1.call-update) | async-done | bytes 262160 | tf_op jit(solution)/shard_map/reduce_scatter | solution.py:79
  (13 shorter events, 0.1 us)
Async XLA Ops:
  7.2 238.7 %copy-start = (bf16[512,512]{1,0:T(8,128)(2,1)S(1)}, bf16[512,512]{1,0:T(8,128)(2,1)}, u32[]{:S(2)}) copy-start(bf16[512,512]{1,0:T(8,128)(2,1)} %param.12) | copy-start | bytes 1572868
  7.2 55.1 %copy-start.1 = (s32[256]{0:T(256)S(1)}, s32[256]{0:T(256)}, u32[]{:S(2)}) copy-start(s32[256]{0:T(256)} %param.16) | copy-start | bytes 3076
  7.2 55.1 %copy-start.2 = (s32[256]{0:T(256)S(1)}, s32[256]{0:T(256)}, u32[]{:S(2)}) copy-start(s32[256]{0:T(256)} %param.15) | copy-start | bytes 3076
  7.2 54.8 %all-gather.3.cloned.1.call-start = ((), (), s32[]{:S(2)}) async-start(), calls=%async_computation.1 | async-start | bytes 2359296 | tf_op jit(solution)/shard_map/all_gather | solution.py:50
  7.9 237.9 %all-gather.5.cloned.1.call-start = ((), (), s32[]{:S(2)}) async-start(), calls=%async_computation.2 | async-start | bytes 1310720 | tf_op jit(solution)/shard_map/all_gather | solution.py:64
  8.7 420.2 %all-reduce.3.cloned.1.call-start = ((), (), s32[]{:S(2)}) async-start(), calls=%async_computation.3 | async-start | bytes 2097152 | tf_op jit(solution)/shard_map/psum | solution.py:74
  254.2 350.8 %reduce-scatter.2.cloned.1.call-start = ((), (), s32[]{:S(2)}) async-start(), calls=%async_computation.4 | async-start | bytes 2359296 | tf_op jit(solution)/shard_map/reduce_scatter | solution.py:79
Sparse Core Ops, SparseCore 0:
  10.1 51.7 all-gather.2
  63.5 15.2 all-gather.4
  254.3 174.4 all-reduce.2
  432.8 172.1 reduce-scatter.1
where the time goes:
time: 614 us; the launch traced here: 612 us
  waiting for transfers between devices  277 us (45%)
  other arithmetic  135 us (22%)
  blocking collectives  87.7 us (14%)
  matrix products  65.7 us (11%)
  local copies, waits for them, and re-layouts  31.2 us (5%)
  between operations  14.5 us (2%)
    reduce_scatter x1, waiting for transfers between devices, local(): lax.psum_scatter(contributions.reshape(-1, feature_width).astype(jnp.bflo...  174 us
    psum x1, blocking collectives, local(): aggregate_all = lax.psum(partial_value, 'rep').astype(jnp.bfloat16)  87.7 us
    scatter-add x4, other arithmetic, one_turn(): return totals.at[placed].add(product * (slot_mask * inside)[:, None, None])  73.9 us
    all_gather x1, waiting for transfers between devices, local(): gathered = lax.all_gather(features, 'node', axis=0, tiled=True)  52.6 us
    psum x1, waiting for transfers between devices, local(): weight_grad = lax.psum(weight_term, ('node', 'rep')) * scale  49 us
    scatter-add x4, other arithmetic, one_turn(): return totals.at[rows_here].add(product * slot_mask[:, None, None])  47.1 us
    dot_general x4, matrix products, one_turn(): jnp.einsum('tji,tjf->tif', values, sources[rows_here], preferred_element_...  29.1 us
    dot_general x4, matrix products, one_turn(): jnp.einsum('tij,tjf->tif', values, sources[cols_here], preferred_element_...  28.2 us
  transfers between devices with their start and end apart: 4, of which 3 were waited for; matrix products, arithmetic and copies ran while one was open for 37% of the time, Pallas kernels for 0%

commit v1 on v0

--- a/solution.py
+++ b/solution.py
@@ -60,7 +60,7 @@
         False,
         0,
     ).reshape(block_count * TB, feature_width)
-    aggregate_all = lax.psum(partial_value, "rep").astype(jnp.bfloat16)
+    aggregate_all = jnp.sum(lax.all_gather(partial_value, "rep"), axis=0).astype(jnp.bfloat16)
     cotangent_all = lax.all_gather(cotangent, "rep", axis=0, tiled=True)
     pre = jnp.dot(aggregate_all, weight, preferred_element_type=jnp.float32)
     activated, pullback = jax.vjp(smooth_gate, pre)

time: 614 us -> 649 us (1.057)
  waiting for transfers between devices: 277 us -> 395 us
  blocking collectives: 87.7 us -> 0 us
    all_gather x0 -> x1, waiting for transfers between devices: none -> 149 us  [local(): lax.all_gather(partial_value, 'rep')]
    psum x1 -> x0, blocking collectives: 87.7 us -> none  [local(): aggregate_all = lax.psum(partial_value, 'rep').astype(jnp.bfloat16)]
    psum x1, waiting for transfers between devices: 49 us -> 5.2 us  [local(): weight_grad = lax.psum(weight_term, ('node', 'rep')) * scale]
    all_gather x1, waiting for transfers between devices: 0.01 us -> 13.7 us  [local(): cotangent_all = lax.all_gather(cotangent, 'rep', axis=0, tiled=True)]
  transfers between devices with their start and end apart: 4 -> 5, of which waited for: 3 -> 5; matrix products, arithmetic and copies ran while one was open for 37% -> 20% of each run, Pallas kernels for 0% -> 0%
where the time goes in v1:
time: 649 us; the launch traced here: 646 us
  waiting for transfers between devices  395 us (61%)
  other arithmetic  140 us (22%)
  matrix products  64.1 us (10%)
  local copies, waits for them, and re-layouts  32.7 us (5%)
  between operations  14.5 us (2%)
    reduce_scatter x1, waiting for transfers between devices, local(): lax.psum_scatter(contributions.reshape(-1, feature_width).astype(jnp.bflo...  172 us
    all_gather x1, waiting for transfers between devices, local(): lax.all_gather(partial_value, 'rep')  149 us
    scatter-add x4, other arithmetic, one_turn(): return totals.at[placed].add(product * (slot_mask * inside)[:, None, None])  73.8 us
    all_gather x1, waiting for transfers between devices, local(): gathered = lax.all_gather(features, 'node', axis=0, tiled=True)  53.3 us
    scatter-add x4, other arithmetic, one_turn(): return totals.at[rows_here].add(product * slot_mask[:, None, None])  47.1 us
    dot_general x4, matrix products, one_turn(): jnp.einsum('tji,tjf->tif', values, sources[rows_here], preferred_element_...  29.1 us
    dot_general x4, matrix products, one_turn(): jnp.einsum('tij,tjf->tif', values, sources[cols_here], preferred_element_...  27.9 us
    gather x4, local copies, waits for them, and re-layouts, one_turn(): sources[cols_here]  17.5 us
  transfers between devices with their start and end apart: 5, of which 5 were waited for; matrix products, arithmetic and copies ran while one was open for 20% of the time, Pallas kernels for 0%

profile of v1, /device:TPU:0, one launch (start us, length us, event | category | flops | bytes accessed | tf_op | source)
XLA Modules:
  0.0 646.3 jit_solution(16538690188308362931)
XLA Ops:
  7.2 0.0 all-gather.4.cloned.1.call-start
  7.2 0.7 all-gather.4.cloned.1.call-update
  7.9 0.0 all-gather.6.cloned.1.call-start
  8.6 53.3 %all-gather.4.cloned.1.call-done = bf16[2048,512]{1,0:T(8,128)(2,1)} async-done(((bf16[256,512]{1,0:T(8,128)(2,1)}), bf16[2048,512]{1,0:T(8,128)(2,1)}) %all-gather.4.cloned.1.call-update) | async-done | bytes 2097168 | tf_op jit(solution)/shard_map/all_gather | solution.py:50
  62.0 0.2 broadcast_in_dim.20
  62.3 95.7 %while.20 = (s32[]{:T(128)}, f32[8,128,512]{2,1,0:T(8,128)S(1)}, s32[]{:T(128)}, s32[256]{0:T(256)S(1)}, bf16[256,128,128]{2,1,0:T(8,128)(2,1)}, /*index=5*/s32[...) while((s32[]{:T(128)}, f32[8,128,512]{2,1,0:T(8,128)S(1)}, ...), condition=%wide.region_2.3_spmd, body=%wide.region_0.2_spmd.sunk | while | flops 541066560 | bytes 47191344 | solution.py:41
  62.3 0.7 compare_convert_fusion.3
  62.9 0.1 compare_select_fusion.6
  63.0 4.4 gather_fusion
  67.4 7.0 %broadcast_multiply_fusion.5 = f32[32,128,512]{2,1,0:T(8,128)} fusion(f32[32]{0:T(128)S(1)} %compare_convert_fusion.3, bf16[32,128,512]{2,1,0:T(8,128)(2,1)} %gather_fusion, bf16[256,128,128]{2,1,0:T(8,128)(2,1)} %get-tuple-element.282, s32[]{:T(128)S(6)} %select_n.44), kind=kOutput, calls=%fused_computation.4.clone.1 | convolution fusion | flops 538968064 | bytes 13631620 | tf_op jit(solution)/shard_map/while/body/tij,tjf->tif/dot_general | solution.py:36
  74.4 11.7 %scatter_fusion = f32[8,128,512]{2,1,0:T(8,128)S(1)} fusion(f32[8,128,512]{2,1,0:T(8,128)S(1)} %get-tuple-element.267, s32[32]{0:T(128)S(1)} %get-tuple-element.242, f32[32,128,512]{2,1,0:T(8,128)} %broadcast_multiply_fusion.5), kind=kCustom, calls=%fused_computation.2.clone.1 | custom fusion | flops 2097152 | bytes 25165952 | tf_op jit(solution)/shard_map/while/body/scatter-add | solution.py:39
  86.2 0.7 compare_convert_fusion.3
  86.8 0.1 compare_select_fusion.6
  86.9 4.4 gather_fusion
  91.3 7.0 %broadcast_multiply_fusion.5 = f32[32,128,512]{2,1,0:T(8,128)} fusion(f32[32]{0:T(128)S(1)} %compare_convert_fusion.3, bf16[32,128,512]{2,1,0:T(8,128)(2,1)} %gather_fusion, bf16[256,128,128]{2,1,0:T(8,128)(2,1)} %get-tuple-element.282, s32[]{:T(128)S(6)} %select_n.44), kind=kOutput, calls=%fused_computation.4.clone.1 | convolution fusion | flops 538968064 | bytes 13631620 | tf_op jit(solution)/shard_map/while/body/tij,tjf->tif/dot_general | solution.py:36
  98.3 11.8 %scatter_fusion = f32[8,128,512]{2,1,0:T(8,128)S(1)} fusion(f32[8,128,512]{2,1,0:T(8,128)S(1)} %get-tuple-element.267, s32[32]{0:T(128)S(1)} %get-tuple-element.242, f32[32,128,512]{2,1,0:T(8,128)} %broadcast_multiply_fusion.5), kind=kCustom, calls=%fused_computation.2.clone.1 | custom fusion | flops 2097152 | bytes 25165952 | tf_op jit(solution)/shard_map/while/body/scatter-add | solution.py:39
  110.1 0.7 compare_convert_fusion.3
  110.7 0.1 compare_select_fusion.6
  110.8 4.4 gather_fusion
  115.2 7.0 %broadcast_multiply_fusion.5 = f32[32,128,512]{2,1,0:T(8,128)} fusion(f32[32]{0:T(128)S(1)} %compare_convert_fusion.3, bf16[32,128,512]{2,1,0:T(8,128)(2,1)} %gather_fusion, bf16[256,128,128]{2,1,0:T(8,128)(2,1)} %get-tuple-element.282, s32[]{:T(128)S(6)} %select_n.44), kind=kOutput, calls=%fused_computation.4.clone.1 | convolution fusion | flops 538968064 | bytes 13631620 | tf_op jit(solution)/shard_map/while/body/tij,tjf->tif/dot_general | solution.py:36
  122.2 11.7 %scatter_fusion = f32[8,128,512]{2,1,0:T(8,128)S(1)} fusion(f32[8,128,512]{2,1,0:T(8,128)S(1)} %get-tuple-element.267, s32[32]{0:T(128)S(1)} %get-tuple-element.242, f32[32,128,512]{2,1,0:T(8,128)} %broadcast_multiply_fusion.5), kind=kCustom, calls=%fused_computation.2.clone.1 | custom fusion | flops 2097152 | bytes 25165952 | tf_op jit(solution)/shard_map/while/body/scatter-add | solution.py:39
  134.0 0.7 compare_convert_fusion.3
  134.6 0.1 compare_select_fusion.6
  134.7 4.4 gather_fusion
  139.1 7.0 %broadcast_multiply_fusion.5 = f32[32,128,512]{2,1,0:T(8,128)} fusion(f32[32]{0:T(128)S(1)} %compare_convert_fusion.3, bf16[32,128,512]{2,1,0:T(8,128)(2,1)} %gather_fusion, bf16[256,128,128]{2,1,0:T(8,128)(2,1)} %get-tuple-element.282, s32[]{:T(128)S(6)} %select_n.44), kind=kOutput, calls=%fused_computation.4.clone.1 | convolution fusion | flops 538968064 | bytes 13631620 | tf_op jit(solution)/shard_map/while/body/tij,tjf->tif/dot_general | solution.py:36
  146.1 11.8 %scatter_fusion = f32[8,128,512]{2,1,0:T(8,128)S(1)} fusion(f32[8,128,512]{2,1,0:T(8,128)S(1)} %get-tuple-element.267, s32[32]{0:T(128)S(1)} %get-tuple-element.242, f32[32,128,512]{2,1,0:T(8,128)} %broadcast_multiply_fusion.5), kind=kCustom, calls=%fused_computation.2.clone.1 | custom fusion | flops 2097152 | bytes 25165952 | tf_op jit(solution)/shard_map/while/body/scatter-add | solution.py:39
  157.9 1.4 copy-done.1
  159.3 0.0 all-gather.8.cloned.1.call-start
  159.4 0.7 all-gather.8.cloned.1.call-update
  160.0 0.0 all-reduce.2.cloned.1.call-start
  160.1 148.7 %all-gather.6.cloned.1.call-done = f32[4,1024,512]{2,1,0:T(8,128)} async-done(((f32[1,1024,512]{2,1,0:T(8,128)}), f32[4,1024,512]{2,1,0:T(8,128)}) %all-gather.6.cloned.1.call-update) | async-done | bytes 8388624 | tf_op jit(solution)/shard_map/all_gather | solution.py:63
  308.8 4.6 reduce_sum.9
  313.4 13.7 %all-gather.8.cloned.1.call-done = bf16[1024,512]{1,0:T(8,128)(2,1)} async-done(((bf16[256,512]{1,0:T(8,128)(2,1)}), bf16[1024,512]{1,0:T(8,128)(2,1)}) %all-gather.8.cloned.1.call-update) | async-done | bytes 1048592 | tf_op jit(solution)/shard_map/all_gather | solution.py:64
  327.1 5.0 fusion.6
  332.1 0.7 convolution_convert_fusion
  332.9 1.3 fusion.15
  334.2 0.0 reduce-scatter.2.cloned.1.call-start
  334.2 2.5 broadcast_in_dim.21
  336.7 117.2 %while.21 = (s32[]{:T(128)}, f32[16,128,512]{2,1,0:T(8,128)}, s32[]{:T(128)}, s32[256]{0:T(256)S(1)}, bf16[256,128,128]{2,1,0:T(8,128)(2,1)}, /*index=5*/s32[256...) while((s32[]{:T(128)}, f32[16,128,512]{2,1,0:T(8,128)}, ...), condition=%wide.region_7.8_spmd, body=%wide.region_5.7_spmd.sunk | while | flops 541066688 | bytes 47191480 | solution.py:41
  336.7 0.7 and_select_fusion.2
  337.4 0.1 compare_select_fusion.7
  337.5 2.8 gather_fusion.1
  340.3 7.3 %broadcast_multiply_fusion.6 = f32[32,128,512]{2,1,0:T(8,128)} fusion(f32[32]{0:T(128)S(1)} %and_select_fusion.2, bf16[32,128,512]{2,1,0:T(8,128)(2,1)} %gather_fusion.1, bf16[256,128,128]{2,1,0:T(8,128)(2,1)} %get-tuple-element.318, s32[]{:T(128)S(6)} %select_n.46), kind=kOutput, calls=%fused_computation.11.clone.1 | convolution fusion | flops 538968064 | bytes 13631620 | tf_op jit(solution)/shard_map/while/body/tji,tjf->tif/dot_general | solution.py:32
  347.6 18.5 %scatter_fusion.1 = f32[16,128,512]{2,1,0:T(8,128)} fusion(f32[16,128,512]{2,1,0:T(8,128)} %get-tuple-element.303, s32[32]{0:T(128)S(1)} %get-tuple-element.252, f32[32,128,512]{2,1,0:T(8,128)} %broadcast_multiply_fusion.6), kind=kCustom, calls=%fused_computation.3.clone.1 | custom fusion | flops 2097152 | bytes 25165952 | tf_op jit(solution)/shard_map/while/body/scatter-add | solution.py:35
  366.0 0.7 and_select_fusion.2
  366.8 0.1 compare_select_fusion.7
  366.8 2.8 gather_fusion.1
  369.6 7.3 %broadcast_multiply_fusion.6 = f32[32,128,512]{2,1,0:T(8,128)} fusion(f32[32]{0:T(128)S(1)} %and_select_fusion.2, bf16[32,128,512]{2,1,0:T(8,128)(2,1)} %gather_fusion.1, bf16[256,128,128]{2,1,0:T(8,128)(2,1)} %get-tuple-element.318, s32[]{:T(128)S(6)} %select_n.46), kind=kOutput, calls=%fused_computation.11.clone.1 | convolution fusion | flops 538968064 | bytes 13631620 | tf_op jit(solution)/shard_map/while/body/tji,tjf->tif/dot_general | solution.py:32
  376.9 18.5 %scatter_fusion.1 = f32[16,128,512]{2,1,0:T(8,128)} fusion(f32[16,128,512]{2,1,0:T(8,128)} %get-tuple-element.303, s32[32]{0:T(128)S(1)} %get-tuple-element.252, f32[32,128,512]{2,1,0:T(8,128)} %broadcast_multiply_fusion.6), kind=kCustom, calls=%fused_computation.3.clone.1 | custom fusion | flops 2097152 | bytes 25165952 | tf_op jit(solution)/shard_map/while/body/scatter-add | solution.py:35
  395.4 0.7 and_select_fusion.2
  396.2 0.1 compare_select_fusion.7
  396.2 2.8 gather_fusion.1
  399.0 7.3 %broadcast_multiply_fusion.6 = f32[32,128,512]{2,1,0:T(8,128)} fusion(f32[32]{0:T(128)S(1)} %and_select_fusion.2, bf16[32,128,512]{2,1,0:T(8,128)(2,1)} %gather_fusion.1, bf16[256,128,128]{2,1,0:T(8,128)(2,1)} %get-tuple-element.318, s32[]{:T(128)S(6)} %select_n.46), kind=kOutput, calls=%fused_computation.11.clone.1 | convolution fusion | flops 538968064 | bytes 13631620 | tf_op jit(solution)/shard_map/while/body/tji,tjf->tif/dot_general | solution.py:32
  406.3 18.3 %scatter_fusion.1 = f32[16,128,512]{2,1,0:T(8,128)} fusion(f32[16,128,512]{2,1,0:T(8,128)} %get-tuple-element.303, s32[32]{0:T(128)S(1)} %get-tuple-element.252, f32[32,128,512]{2,1,0:T(8,128)} %broadcast_multiply_fusion.6), kind=kCustom, calls=%fused_computation.3.clone.1 | custom fusion | flops 2097152 | bytes 25165952 | tf_op jit(solution)/shard_map/while/body/scatter-add | solution.py:35
  424.6 0.7 and_select_fusion.2
  425.3 0.1 compare_select_fusion.7
  425.4 2.8 gather_fusion.1
  428.1 7.3 %broadcast_multiply_fusion.6 = f32[32,128,512]{2,1,0:T(8,128)} fusion(f32[32]{0:T(128)S(1)} %and_select_fusion.2, bf16[32,128,512]{2,1,0:T(8,128)(2,1)} %gather_fusion.1, bf16[256,128,128]{2,1,0:T(8,128)(2,1)} %get-tuple-element.318, s32[]{:T(128)S(6)} %select_n.46), kind=kOutput, calls=%fused_computation.11.clone.1 | convolution fusion | flops 538968064 | bytes 13631620 | tf_op jit(solution)/shard_map/while/body/tji,tjf->tif/dot_general | solution.py:32
  435.4 18.5 %scatter_fusion.1 = f32[16,128,512]{2,1,0:T(8,128)} fusion(f32[16,128,512]{2,1,0:T(8,128)} %get-tuple-element.303, s32[32]{0:T(128)S(1)} %get-tuple-element.252, f32[32,128,512]{2,1,0:T(8,128)} %broadcast_multiply_fusion.6), kind=kCustom, calls=%fused_computation.3.clone.1 | custom fusion | flops 2097152 | bytes 25165952 | tf_op jit(solution)/shard_map/while/body/scatter-add | solution.py:35
  453.9 3.8 convert_element_type.37
  457.8 2.0 fusion.14
  459.8 5.2 all-reduce.2.cloned.1.call-done
  465.0 2.3 broadcast_multiply_fusion.2
  467.3 172.5 %reduce-scatter.2.cloned.1.call-done = bf16[256,512]{1,0:T(8,128)(2,1)} async-done(((bf16[2048,512]{1,0:T(8,128)(2,1)}), bf16[256,512]{1,0:T(8,128)(2,1)}) %reduce-scatter.2.cloned.1.call-update) | async-done | bytes 262160 | tf_op jit(solution)/shard_map/reduce_scatter | solution.py:79
  (18 shorter events, 0.1 us)
Async XLA Ops:
  7.2 319.9 %copy-start = (bf16[512,512]{1,0:T(8,128)(2,1)S(1)}, bf16[512,512]{1,0:T(8,128)(2,1)}, u32[]{:S(2)}) copy-start(bf16[512,512]{1,0:T(8,128)(2,1)} %param.12) | copy-start | bytes 1572868
  7.2 55.1 %copy-start.2 = (s32[256]{0:T(256)S(1)}, s32[256]{0:T(256)}, u32[]{:S(2)}) copy-start(s32[256]{0:T(256)} %param.16) | copy-start | bytes 3076
  7.2 55.1 %copy-start.3 = (s32[256]{0:T(256)S(1)}, s32[256]{0:T(256)}, u32[]{:S(2)}) copy-start(s32[256]{0:T(256)} %param.15) | copy-start | bytes 3076
  7.2 54.8 %all-gather.4.cloned.1.call-start = ((), (), s32[]{:S(2)}) async-start(), calls=%async_computation.1 | async-start | bytes 2359296 | tf_op jit(solution)/shard_map/all_gather | solution.py:50
  7.9 300.9 %all-gather.6.cloned.1.call-start = ((), (), s32[]{:S(2)}) async-start(), calls=%async_computation.2 | async-start | bytes 10485760 | tf_op jit(solution)/shard_map/all_gather | solution.py:63
  157.9 1.4 copy-start.1
  159.3 167.8 %all-gather.8.cloned.1.call-start = ((), (), s32[]{:S(2)}) async-start(), calls=%async_computation.3 | async-start | bytes 1310720 | tf_op jit(solution)/shard_map/all_gather | solution.py:64
  160.0 304.9 %all-reduce.2.cloned.1.call-start = ((), (), s32[]{:S(2)}) async-start(), calls=%async_computation.4 | async-start | bytes 2097152 | tf_op jit(solution)/shard_map/psum | solution.py:74
  334.2 305.6 %reduce-scatter.2.cloned.1.call-start = ((), (), s32[]{:S(2)}) async-start(), calls=%async_computation.5 | async-start | bytes 2359296 | tf_op jit(solution)/shard_map/reduce_scatter | solution.py:79
Sparse Core Ops, SparseCore 0:
  10.1 51.7 all-gather.3
  159.4 149.3 all-gather.5
  310.4 16.6 all-gather.7
  334.3 130.6 all-reduce.1
  468.9 170.8 reduce-scatter.1
